TPU v7x, 512 devices: a whole 4x4x16 slice. The times are simulated.
512 devices in a mesh: space: 128 (over z, y, x_lo), shot: 4 (over x_hi, core).
Axes of the slice: x: 4 (x_hi: 2, x_lo: 2; x = x_hi * 2 + x_lo), y: 4, z: 16, core: 2. Of those that a mesh axis runs over, the one named last changes fastest.
Arguments:
- velocity: float32 [1024, 192, 128], P('space'), may hold values from 1.5 to 4.5
- wave_now: float32 [4, 1024, 192, 128], P('shot', 'space'), may hold values from -6 to 6
- wave_prev: float32 [4, 1024, 192, 128], P('shot', 'space'), may hold values from -6 to 6
- adjoint_now: float32 [4, 1024, 192, 128], P('shot', 'space'), may hold values from -6 to 6
- adjoint_prev: float32 [4, 1024, 192, 128], P('shot', 'space'), may hold values from -6 to 6
- source_cells: int32 [4, 128], P('shot'), may hold values from 0 to 25165823, as said below
- wavelet: float32 [4, 10, 128], P('shot'), may hold values from -24 to 24
- receiver_cells: int32 [65536], P('space'), may hold values from 0 to 196607, as said below
- receiver_counts: int32 [128], P('space'), may hold values from 128 to 512, as said below
- observed: float32 [4, 10, 65536], P('shot', None, 'space'), may hold values from -24 to 24
Outputs:
- gradient: float32 [1024, 192, 128], P('space', 'shot')
Inputs may be any that keep to these rules, and one draw needn't show every extreme that they name: `source_cells`: flat indices into the whole grid (first dimension slowest); the 128 cells of one shot group are distinct. `receiver_cells`: flat indices within one device's block of 8 x 192 x 128 cells (first dimension slowest); the 512 cells of one block are distinct. `receiver_counts`: the live slots of a block come first.
All inputs are finite; a program needn't handle non-finite values.
Results may differ from a plain program's by a relative error of at most 0.00002.
Values sent between devices are 32-bit elements; how exact they have to be, the bound alone decides.
No kernel may reach another device: no remote copies, remote signals or barrier semaphores. Data moves between devices by JAX's collectives and lax.ppermute only.
A program may use at most 64 MiB of HBM per device.

v0:
```python
import jax
import jax.numpy as jnp
from jax import lax
from jax.sharding import PartitionSpec as P

TAPS = (-205.0 / 72.0, 8.0 / 5.0, -1.0 / 5.0, 8.0 / 315.0, -1.0 / 560.0)
COURANT = 0.09


def with_halo(block, sides, width):
    for axis, dim in sides:
        count = lax.axis_size(axis)
        forward = [(i, i + 1) for i in range(count - 1)]
        backward = [(target, source) for source, target in forward]
        low = lax.ppermute(
            lax.slice_in_dim(block, block.shape[dim] - width, None, axis=dim), axis, forward
        )
        high = lax.ppermute(lax.slice_in_dim(block, 0, width, axis=dim), axis, backward)
        block = jnp.concatenate([low, block, high], axis=dim)
    return block


def laplace(widened):
    length_x = widened.shape[0] - 8
    extent_y = widened.shape[1]
    extent_z = widened.shape[2]
    padded = jnp.pad(widened, ((0, 0), (4, 4), (4, 4)))
    centre = widened[4 : 4 + length_x]
    result = 3.0 * TAPS[0] * centre
    for distance in range(1, 5):
        beside_all = (
            padded[4 + distance : 4 + distance + length_x, 4 : 4 + extent_y, 4 : 4 + extent_z]
            + padded[4 - distance : 4 - distance + length_x, 4 : 4 + extent_y, 4 : 4 + extent_z]
        )
        beside_all = (
            beside_all
            + padded[4 : 4 + length_x, 4 + distance : 4 + distance + extent_y, 4 : 4 + extent_z]
            + padded[4 : 4 + length_x, 4 - distance : 4 - distance + extent_y, 4 : 4 + extent_z]
        )
        beside_all = (
            beside_all
            + padded[4 : 4 + length_x, 4 : 4 + extent_y, 4 + distance : 4 + distance + extent_z]
            + padded[4 : 4 + length_x, 4 : 4 + extent_y, 4 - distance : 4 - distance + extent_z]
        )
        result = result + TAPS[distance] * beside_all
    return result


def edge_layers(field):
    return with_halo(field, (("space", 0),), 4)


def add_at(field, target, amounts):
    size_all = field.size
    inside = (target >= 0) & (target < size_all)
    flat_field = (
        field.reshape(-1).at[jnp.where(inside, target, 0)].add(jnp.where(inside, amounts, 0.0))
    )
    return flat_field.reshape(field.shape)


def per_device(
    velocity,
    wave_now,
    wave_prev,
    adjoint_now,
    adjoint_prev,
    source_cells,
    wavelet,
    receiver_cells,
    receiver_counts,
    observed,
):
    extent_x, extent_y, extent_z = velocity.shape
    plane_cells = extent_y * extent_z
    courant_sq = (COURANT * velocity) ** 2
    position = lax.axis_index("space")
    local_sources = source_cells[0] - position * (extent_x * plane_cells)
    pulses = wavelet[0]

    def forward(carried, source_pulse):
        current, former = carried
        latest = 2.0 * current - former + courant_sq * laplace(edge_layers(current))
        latest = add_at(latest, local_sources, source_pulse)
        acceleration = latest - 2.0 * current + former
        return ((latest, current), (acceleration, latest.reshape(-1)[receiver_cells]))

    _, (accelerations, traces) = lax.scan(forward, (wave_now[0], wave_prev[0]), pulses)
    live_slots = (jnp.arange(receiver_cells.shape[0], dtype=jnp.int32) < receiver_counts[0]).astype(
        jnp.float32
    )
    misfit = (traces - observed[0]) * live_slots

    def backward(carried, inputs):
        following, furthest, imaging = carried
        acceleration, residual = inputs
        earlier = 2.0 * following - furthest + courant_sq * laplace(edge_layers(following))
        earlier = earlier.reshape(-1).at[receiver_cells].add(residual).reshape(velocity.shape)
        return ((earlier, following, imaging + earlier * acceleration), None)

    empty_field = jnp.zeros_like(velocity)
    (_, _, imaging), _ = lax.scan(
        backward,
        (adjoint_now[0], adjoint_prev[0], empty_field),
        (accelerations, misfit),
        reverse=True,
    )
    band_rows = extent_y // lax.axis_size("shot")
    offset = lax.axis_index("shot") * band_rows
    factor = lax.dynamic_slice_in_dim(-2.0 / velocity**3, offset, band_rows, 1)
    summed = lax.psum(imaging, "shot")
    own_band = lax.dynamic_slice_in_dim(summed, offset, band_rows, 1)
    return factor * own_band


def solution(mesh):
    in_specs = (
        P("space", None, None),
        P("shot", "space", None, None),
        P("shot", "space", None, None),
        P("shot", "space", None, None),
        P("shot", "space", None, None),
        P("shot", None),
        P("shot", None, None),
        P("space"),
        P("space"),
        P("shot", None, "space"),
    )
    out_specs = P("space", "shot", None)
    return jax.shard_map(
        per_device, mesh=mesh, in_specs=in_specs, out_specs=out_specs, check_vma=False
    )
```

profile of v0, /device:TPU:1, one launch (start us, length us, event | category | flops | bytes accessed | tf_op | source)
XLA Modules:
  0.0 773.0 jit_solution(16620281286347901368)
XLA Ops:
  12.2 333.3 %while.37 = (s32[]{:T(128)}, f32[8,192,128]{2,1,0:T(8,128)S(1)}, f32[8,192,128]{2,1,0:T(8,128)}, f32[10,8,192,128]{3,2,1,0:T(8,128)}, f32[10,512]{1,0:T(8,128)},...) while((s32[]{:T(128)}, f32[8,192,128]{2,1,0:T(8,128)S(1)}, ...), condition=%wide.region_2.3_spmd, body=%wide.region_0.2_spmd.sunk | while | flops 13609986 | bytes 43449096 | solution.py:88
  13.0 4.0 collective-permute-start.1
  22.2 13.2 %collective-permute-done = f32[4,192,128]{2,1,0:T(8,128)S(1)} collective-permute-done((f32[4,192,128]{2,1,0:T(8,128)S(1)}, f32[4,192,128]{2,1,0:T(8,128)S(1)}, u32[]{:S(2)}, u32[]{:S(2)}) %collective-permute-start) | collective-permute-done | bytes 393248 | tf_op jit(solution)/shard_map/while/body/eval_jaxpr/ppermute | solution.py:18
  56.1 4.0 collective-permute-done.1
  60.3 10.1 %collective-permute-done = f32[4,192,128]{2,1,0:T(8,128)S(1)} collective-permute-done((f32[4,192,128]{2,1,0:T(8,128)S(1)}, f32[4,192,128]{2,1,0:T(8,128)S(1)}, u32[]{:S(2)}, u32[]{:S(2)}) %collective-permute-start) | collective-permute-done | bytes 393248 | tf_op jit(solution)/shard_map/while/body/eval_jaxpr/ppermute | solution.py:18
  94.5 9.8 %collective-permute-done = f32[4,192,128]{2,1,0:T(8,128)S(1)} collective-permute-done((f32[4,192,128]{2,1,0:T(8,128)S(1)}, f32[4,192,128]{2,1,0:T(8,128)S(1)}, u32[]{:S(2)}, u32[]{:S(2)}) %collective-permute-start) | collective-permute-done | bytes 393248 | tf_op jit(solution)/shard_map/while/body/eval_jaxpr/ppermute | solution.py:18
  127.4 9.7 %collective-permute-done = f32[4,192,128]{2,1,0:T(8,128)S(1)} collective-permute-done((f32[4,192,128]{2,1,0:T(8,128)S(1)}, f32[4,192,128]{2,1,0:T(8,128)S(1)}, u32[]{:S(2)}, u32[]{:S(2)}) %collective-permute-start) | collective-permute-done | bytes 393248 | tf_op jit(solution)/shard_map/while/body/eval_jaxpr/ppermute | solution.py:18
  159.2 8.4 %collective-permute-done = f32[4,192,128]{2,1,0:T(8,128)S(1)} collective-permute-done((f32[4,192,128]{2,1,0:T(8,128)S(1)}, f32[4,192,128]{2,1,0:T(8,128)S(1)}, u32[]{:S(2)}, u32[]{:S(2)}) %collective-permute-start) | collective-permute-done | bytes 393248 | tf_op jit(solution)/shard_map/while/body/eval_jaxpr/ppermute | solution.py:18
  190.1 8.0 %collective-permute-done = f32[4,192,128]{2,1,0:T(8,128)S(1)} collective-permute-done((f32[4,192,128]{2,1,0:T(8,128)S(1)}, f32[4,192,128]{2,1,0:T(8,128)S(1)}, u32[]{:S(2)}, u32[]{:S(2)}) %collective-permute-start) | collective-permute-done | bytes 393248 | tf_op jit(solution)/shard_map/while/body/eval_jaxpr/ppermute | solution.py:18
  219.2 5.9 collective-permute-done
  245.8 4.1 collective-permute-done.1
  250.1 10.8 %collective-permute-done = f32[4,192,128]{2,1,0:T(8,128)S(1)} collective-permute-done((f32[4,192,128]{2,1,0:T(8,128)S(1)}, f32[4,192,128]{2,1,0:T(8,128)S(1)}, u32[]{:S(2)}, u32[]{:S(2)}) %collective-permute-start) | collective-permute-done | bytes 393248 | tf_op jit(solution)/shard_map/while/body/eval_jaxpr/ppermute | solution.py:18
  275.3 5.2 collective-permute-start.1
  285.8 11.1 %collective-permute-done = f32[4,192,128]{2,1,0:T(8,128)S(1)} collective-permute-done((f32[4,192,128]{2,1,0:T(8,128)S(1)}, f32[4,192,128]{2,1,0:T(8,128)S(1)}, u32[]{:S(2)}, u32[]{:S(2)}) %collective-permute-start) | collective-permute-done | bytes 393248 | tf_op jit(solution)/shard_map/while/body/eval_jaxpr/ppermute | solution.py:18
  311.3 5.2 collective-permute-start.1
  321.8 10.1 %collective-permute-done = f32[4,192,128]{2,1,0:T(8,128)S(1)} collective-permute-done((f32[4,192,128]{2,1,0:T(8,128)S(1)}, f32[4,192,128]{2,1,0:T(8,128)S(1)}, u32[]{:S(2)}, u32[]{:S(2)}) %collective-permute-start) | collective-permute-done | bytes 393248 | tf_op jit(solution)/shard_map/while/body/eval_jaxpr/ppermute | solution.py:18
  346.9 325.5 %while.38 = (s32[]{:T(128)}, f32[8,192,128]{2,1,0:T(8,128)S(1)}, f32[8,192,128]{2,1,0:T(8,128)}, f32[8,192,128]{2,1,0:T(8,128)}, f32[8,192,128]{2,1,0:T(8,128)S(...) while((s32[]{:T(128)}, f32[8,192,128]{2,1,0:T(8,128)S(1)}, ...), condition=%wide.region_5.6_spmd.clone, body=%wide.region_3.5_spmd.clone.sunk | while | flops 13607940 | bytes 49729836 | solution.py:102
  347.0 4.9 collective-permute-start.3
  357.0 6.4 collective-permute-done.2
  375.0 5.3 collective-permute-start.3
  382.4 12.6 %collective-permute-done.3 = f32[4,192,128]{2,1,0:T(8,128)S(1)} collective-permute-done((f32[4,192,128]{2,1,0:T(8,128)S(1)}, f32[4,192,128]{2,1,0:T(8,128)S(1)}, u32[]{:S(2)}, u32[]{:S(2)}) %collective-permute-start.3) | collective-permute-done | bytes 393248 | tf_op jit(solution)/shard_map/while/body/eval_jaxpr/ppermute | solution.py:15
  395.2 5.2 collective-permute-done.2
  412.1 5.3 collective-permute-start.3
  422.9 10.5 %collective-permute-done.2 = f32[4,192,128]{2,1,0:T(8,128)S(1)} collective-permute-done((f32[4,192,128]{2,1,0:T(8,128)S(1)}, f32[4,192,128]{2,1,0:T(8,128)S(1)}, u32[]{:S(2)}, u32[]{:S(2)}) %collective-permute-start.2) | collective-permute-done | bytes 393248 | tf_op jit(solution)/shard_map/while/body/eval_jaxpr/ppermute | solution.py:18
  445.0 5.2 collective-permute-start.3
  452.3 5.2 collective-permute-done.3
  457.7 7.9 %collective-permute-done.2 = f32[4,192,128]{2,1,0:T(8,128)S(1)} collective-permute-done((f32[4,192,128]{2,1,0:T(8,128)S(1)}, f32[4,192,128]{2,1,0:T(8,128)S(1)}, u32[]{:S(2)}, u32[]{:S(2)}) %collective-permute-start.2) | collective-permute-done | bytes 393248 | tf_op jit(solution)/shard_map/while/body/eval_jaxpr/ppermute | solution.py:18
  470.8 3.7 scatter_fusion.1
  477.3 5.3 collective-permute-start.3
  484.7 5.9 collective-permute-done.3
  505.8 4.7 collective-permute-start.3
  512.5 12.5 %collective-permute-done.3 = f32[4,192,128]{2,1,0:T(8,128)S(1)} collective-permute-done((f32[4,192,128]{2,1,0:T(8,128)S(1)}, f32[4,192,128]{2,1,0:T(8,128)S(1)}, u32[]{:S(2)}, u32[]{:S(2)}) %collective-permute-start.3) | collective-permute-done | bytes 393248 | tf_op jit(solution)/shard_map/while/body/eval_jaxpr/ppermute | solution.py:15
  525.3 5.4 collective-permute-done.2
  535.9 3.7 scatter_fusion.1
  542.4 5.0 collective-permute-start.3
  553.0 10.7 %collective-permute-done.2 = f32[4,192,128]{2,1,0:T(8,128)S(1)} collective-permute-done((f32[4,192,128]{2,1,0:T(8,128)S(1)}, f32[4,192,128]{2,1,0:T(8,128)S(1)}, u32[]{:S(2)}, u32[]{:S(2)}) %collective-permute-start.2) | collective-permute-done | bytes 393248 | tf_op jit(solution)/shard_map/while/body/eval_jaxpr/ppermute | solution.py:18
  568.9 3.7 scatter_fusion.1
  575.4 5.0 collective-permute-start.3
  582.4 5.3 collective-permute-done.3
  587.8 7.9 %collective-permute-done.2 = f32[4,192,128]{2,1,0:T(8,128)S(1)} collective-permute-done((f32[4,192,128]{2,1,0:T(8,128)S(1)}, f32[4,192,128]{2,1,0:T(8,128)S(1)}, u32[]{:S(2)}, u32[]{:S(2)}) %collective-permute-start.2) | collective-permute-done | bytes 393248 | tf_op jit(solution)/shard_map/while/body/eval_jaxpr/ppermute | solution.py:18
  601.0 3.7 scatter_fusion.1
  607.4 5.3 collective-permute-start.3
  614.8 5.9 collective-permute-done.3
  635.9 4.7 collective-permute-start.3
  642.6 12.6 %collective-permute-done.3 = f32[4,192,128]{2,1,0:T(8,128)S(1)} collective-permute-done((f32[4,192,128]{2,1,0:T(8,128)S(1)}, f32[4,192,128]{2,1,0:T(8,128)S(1)}, u32[]{:S(2)}, u32[]{:S(2)}) %collective-permute-start.3) | collective-permute-done | bytes 393248 | tf_op jit(solution)/shard_map/while/body/eval_jaxpr/ppermute | solution.py:15
  655.4 5.4 collective-permute-done.2
  666.0 3.7 scatter_fusion.1
  672.5 92.0 %all-reduce.4.cloned.1.call-done = f32[8,192,128]{2,1,0:T(8,128)} async-done(((f32[8,192,128]{2,1,0:T(8,128)}), f32[8,192,128]{2,1,0:T(8,128)}) %all-reduce.4.cloned.1.call-update) | async-done | bytes 786448 | tf_op jit(solution)/shard_map/psum | solution.py:111
  (442 shorter events, 356.1 us)
Async XLA Ops:
  6.5 757.9 %all-reduce.4.cloned.1.call-start = ((), (), s32[]{:S(2)}) async-start(), calls=%async_computation | async-start | bytes 1572864 | tf_op jit(solution)/shard_map/psum | solution.py:111
  12.2 334.7 %copy-start.1 = (f32[1,8,192,128]{3,2,1,0:T(8,128)S(1)}, f32[1,8,192,128]{3,2,1,0:T(8,128)}, u32[]{:S(2)}) copy-start(f32[1,8,192,128]{3,2,1,0:T(8,128)} %param.17) | copy-start | bytes 2359300
  13.0 9.0 %collective-permute-start.1 = (f32[4,192,128]{2,1,0:T(8,128)}, f32[4,192,128]{2,1,0:T(8,128)S(1)}, u32[]{:S(2)}, u32[]{:S(2)}) collective-permute-start(f32[4,192,128]{2,1,0:T(8,128)} %get-tuple-element.457), channel_id=1, source_target_pairs={{0,4},{4,8},{8,12},{12,16},{16,20},{20,24},{24,28},{28,32},{32,36}... | collective-permute-start | bytes 1179656 | tf_op jit(solution)/shard_map/while/body/eval_jaxpr/ppermute | solution.py:15
  17.0 18.4 %collective-permute-start = (f32[4,192,128]{2,1,0:T(8,128)S(1)}, f32[4,192,128]{2,1,0:T(8,128)S(1)}, u32[]{:S(2)}, u32[]{:S(2)}) collective-permute-start(f32[4,192,128]{2,1,0:T(8,128)S(1)} %get-tuple-element.456), channel_id=1, source_target_pairs={{4,0},{8,4},{12,8},{16,12},{20,16},{24,20},{28,24},{32,28},{36,32}... | collective-permute-start | bytes 1179656 | tf_op jit(solution)/shard_map/while/body/eval_jaxpr/ppermute | solution.py:18
  22.2 14.2 %copy-start.2 = (f32[8,192,128]{2,1,0:T(8,128)S(1)}, f32[8,192,128]{2,1,0:T(8,128)}, u32[]{:S(2)}) copy-start(f32[8,192,128]{2,1,0:T(8,128)} %get-tuple-element.485) | copy-start | bytes 2359300 | tf_op jit(solution)/shard_map/while
  49.9 10.3 %collective-permute-start.1 = (f32[4,192,128]{2,1,0:T(8,128)}, f32[4,192,128]{2,1,0:T(8,128)S(1)}, u32[]{:S(2)}, u32[]{:S(2)}) collective-permute-start(f32[4,192,128]{2,1,0:T(8,128)} %get-tuple-element.457), channel_id=1, source_target_pairs={{0,4},{4,8},{8,12},{12,16},{16,20},{20,24},{24,28},{28,32},{32,36}... | collective-permute-start | bytes 1179656 | tf_op jit(solution)/shard_map/while/body/eval_jaxpr/ppermute | solution.py:15
  53.0 17.5 %collective-permute-start = (f32[4,192,128]{2,1,0:T(8,128)S(1)}, f32[4,192,128]{2,1,0:T(8,128)S(1)}, u32[]{:S(2)}, u32[]{:S(2)}) collective-permute-start(f32[4,192,128]{2,1,0:T(8,128)S(1)} %get-tuple-element.456), channel_id=1, source_target_pairs={{4,0},{8,4},{12,8},{16,12},{20,16},{24,20},{28,24},{32,28},{36,32}... | collective-permute-start | bytes 1179656 | tf_op jit(solution)/shard_map/while/body/eval_jaxpr/ppermute | solution.py:18
  84.9 9.3 %collective-permute-start.1 = (f32[4,192,128]{2,1,0:T(8,128)}, f32[4,192,128]{2,1,0:T(8,128)S(1)}, u32[]{:S(2)}, u32[]{:S(2)}) collective-permute-start(f32[4,192,128]{2,1,0:T(8,128)} %get-tuple-element.457), channel_id=1, source_target_pairs={{0,4},{4,8},{8,12},{12,16},{16,20},{20,24},{24,28},{28,32},{32,36}... | collective-permute-start | bytes 1179656 | tf_op jit(solution)/shard_map/while/body/eval_jaxpr/ppermute | solution.py:15
  88.1 16.2 %collective-permute-start = (f32[4,192,128]{2,1,0:T(8,128)S(1)}, f32[4,192,128]{2,1,0:T(8,128)S(1)}, u32[]{:S(2)}, u32[]{:S(2)}) collective-permute-start(f32[4,192,128]{2,1,0:T(8,128)S(1)} %get-tuple-element.456), channel_id=1, source_target_pairs={{4,0},{8,4},{12,8},{16,12},{20,16},{24,20},{28,24},{32,28},{36,32}... | collective-permute-start | bytes 1179656 | tf_op jit(solution)/shard_map/while/body/eval_jaxpr/ppermute | solution.py:18
  118.8 8.4 %collective-permute-start.1 = (f32[4,192,128]{2,1,0:T(8,128)}, f32[4,192,128]{2,1,0:T(8,128)S(1)}, u32[]{:S(2)}, u32[]{:S(2)}) collective-permute-start(f32[4,192,128]{2,1,0:T(8,128)} %get-tuple-element.457), channel_id=1, source_target_pairs={{0,4},{4,8},{8,12},{12,16},{16,20},{20,24},{24,28},{28,32},{32,36}... | collective-permute-start | bytes 1179656 | tf_op jit(solution)/shard_map/while/body/eval_jaxpr/ppermute | solution.py:15
  121.9 15.2 %collective-permute-start = (f32[4,192,128]{2,1,0:T(8,128)S(1)}, f32[4,192,128]{2,1,0:T(8,128)S(1)}, u32[]{:S(2)}, u32[]{:S(2)}) collective-permute-start(f32[4,192,128]{2,1,0:T(8,128)S(1)} %get-tuple-element.456), channel_id=1, source_target_pairs={{4,0},{8,4},{12,8},{16,12},{20,16},{24,20},{28,24},{32,28},{36,32}... | collective-permute-start | bytes 1179656 | tf_op jit(solution)/shard_map/while/body/eval_jaxpr/ppermute | solution.py:18
  151.5 7.5 collective-permute-start.1
  154.0 13.6 %collective-permute-start = (f32[4,192,128]{2,1,0:T(8,128)S(1)}, f32[4,192,128]{2,1,0:T(8,128)S(1)}, u32[]{:S(2)}, u32[]{:S(2)}) collective-permute-start(f32[4,192,128]{2,1,0:T(8,128)S(1)} %get-tuple-element.456), channel_id=1, source_target_pairs={{4,0},{8,4},{12,8},{16,12},{20,16},{24,20},{28,24},{32,28},{36,32}... | collective-permute-start | bytes 1179656 | tf_op jit(solution)/shard_map/while/body/eval_jaxpr/ppermute | solution.py:18
  182.1 7.8 %collective-permute-start.1 = (f32[4,192,128]{2,1,0:T(8,128)}, f32[4,192,128]{2,1,0:T(8,128)S(1)}, u32[]{:S(2)}, u32[]{:S(2)}) collective-permute-start(f32[4,192,128]{2,1,0:T(8,128)} %get-tuple-element.457), channel_id=1, source_target_pairs={{0,4},{4,8},{8,12},{12,16},{16,20},{20,24},{24,28},{28,32},{32,36}... | collective-permute-start | bytes 1179656 | tf_op jit(solution)/shard_map/while/body/eval_jaxpr/ppermute | solution.py:15
  184.9 13.2 %collective-permute-start = (f32[4,192,128]{2,1,0:T(8,128)S(1)}, f32[4,192,128]{2,1,0:T(8,128)S(1)}, u32[]{:S(2)}, u32[]{:S(2)}) collective-permute-start(f32[4,192,128]{2,1,0:T(8,128)S(1)} %get-tuple-element.456), channel_id=1, source_target_pairs={{4,0},{8,4},{12,8},{16,12},{20,16},{24,20},{28,24},{32,28},{36,32}... | collective-permute-start | bytes 1179656 | tf_op jit(solution)/shard_map/while/body/eval_jaxpr/ppermute | solution.py:18
  212.5 6.5 collective-permute-start.1
  214.0 11.1 %collective-permute-start = (f32[4,192,128]{2,1,0:T(8,128)S(1)}, f32[4,192,128]{2,1,0:T(8,128)S(1)}, u32[]{:S(2)}, u32[]{:S(2)}) collective-permute-start(f32[4,192,128]{2,1,0:T(8,128)S(1)} %get-tuple-element.456), channel_id=1, source_target_pairs={{4,0},{8,4},{12,8},{16,12},{20,16},{24,20},{28,24},{32,28},{36,32}... | collective-permute-start | bytes 1179656 | tf_op jit(solution)/shard_map/while/body/eval_jaxpr/ppermute | solution.py:18
  239.6 10.3 %collective-permute-start.1 = (f32[4,192,128]{2,1,0:T(8,128)}, f32[4,192,128]{2,1,0:T(8,128)S(1)}, u32[]{:S(2)}, u32[]{:S(2)}) collective-permute-start(f32[4,192,128]{2,1,0:T(8,128)} %get-tuple-element.457), channel_id=1, source_target_pairs={{0,4},{4,8},{8,12},{12,16},{16,20},{20,24},{24,28},{28,32},{32,36}... | collective-permute-start | bytes 1179656 | tf_op jit(solution)/shard_map/while/body/eval_jaxpr/ppermute | solution.py:15
  242.6 18.3 %collective-permute-start = (f32[4,192,128]{2,1,0:T(8,128)S(1)}, f32[4,192,128]{2,1,0:T(8,128)S(1)}, u32[]{:S(2)}, u32[]{:S(2)}) collective-permute-start(f32[4,192,128]{2,1,0:T(8,128)S(1)} %get-tuple-element.456), channel_id=1, source_target_pairs={{4,0},{8,4},{12,8},{16,12},{20,16},{24,20},{28,24},{32,28},{36,32}... | collective-permute-start | bytes 1179656 | tf_op jit(solution)/shard_map/while/body/eval_jaxpr/ppermute | solution.py:18
  250.0 11.8 %copy-start.2 = (f32[8,192,128]{2,1,0:T(8,128)S(1)}, f32[8,192,128]{2,1,0:T(8,128)}, u32[]{:S(2)}) copy-start(f32[8,192,128]{2,1,0:T(8,128)} %get-tuple-element.485) | copy-start | bytes 2359300 | tf_op jit(solution)/shard_map/while
  275.3 10.2 %collective-permute-start.1 = (f32[4,192,128]{2,1,0:T(8,128)}, f32[4,192,128]{2,1,0:T(8,128)S(1)}, u32[]{:S(2)}, u32[]{:S(2)}) collective-permute-start(f32[4,192,128]{2,1,0:T(8,128)} %get-tuple-element.457), channel_id=1, source_target_pairs={{0,4},{4,8},{8,12},{12,16},{16,20},{20,24},{24,28},{28,32},{32,36}... | collective-permute-start | bytes 1179656 | tf_op jit(solution)/shard_map/while/body/eval_jaxpr/ppermute | solution.py:15
  280.6 16.3 %collective-permute-start = (f32[4,192,128]{2,1,0:T(8,128)S(1)}, f32[4,192,128]{2,1,0:T(8,128)S(1)}, u32[]{:S(2)}, u32[]{:S(2)}) collective-permute-start(f32[4,192,128]{2,1,0:T(8,128)S(1)} %get-tuple-element.456), channel_id=1, source_target_pairs={{4,0},{8,4},{12,8},{16,12},{20,16},{24,20},{28,24},{32,28},{36,32}... | collective-permute-start | bytes 1179656 | tf_op jit(solution)/shard_map/while/body/eval_jaxpr/ppermute | solution.py:18
  285.8 12.0 %copy-start.2 = (f32[8,192,128]{2,1,0:T(8,128)S(1)}, f32[8,192,128]{2,1,0:T(8,128)}, u32[]{:S(2)}) copy-start(f32[8,192,128]{2,1,0:T(8,128)} %get-tuple-element.485) | copy-start | bytes 2359300 | tf_op jit(solution)/shard_map/while
  311.3 10.2 %collective-permute-start.1 = (f32[4,192,128]{2,1,0:T(8,128)}, f32[4,192,128]{2,1,0:T(8,128)S(1)}, u32[]{:S(2)}, u32[]{:S(2)}) collective-permute-start(f32[4,192,128]{2,1,0:T(8,128)} %get-tuple-element.457), channel_id=1, source_target_pairs={{0,4},{4,8},{8,12},{12,16},{16,20},{20,24},{24,28},{28,32},{32,36}... | collective-permute-start | bytes 1179656 | tf_op jit(solution)/shard_map/while/body/eval_jaxpr/ppermute | solution.py:15
  316.6 15.3 %collective-permute-start = (f32[4,192,128]{2,1,0:T(8,128)S(1)}, f32[4,192,128]{2,1,0:T(8,128)S(1)}, u32[]{:S(2)}, u32[]{:S(2)}) collective-permute-start(f32[4,192,128]{2,1,0:T(8,128)S(1)} %get-tuple-element.456), channel_id=1, source_target_pairs={{4,0},{8,4},{12,8},{16,12},{20,16},{24,20},{28,24},{32,28},{36,32}... | collective-permute-start | bytes 1179656 | tf_op jit(solution)/shard_map/while/body/eval_jaxpr/ppermute | solution.py:18
  321.8 11.1 %copy-start.2 = (f32[8,192,128]{2,1,0:T(8,128)S(1)}, f32[8,192,128]{2,1,0:T(8,128)}, u32[]{:S(2)}) copy-start(f32[8,192,128]{2,1,0:T(8,128)} %get-tuple-element.485) | copy-start | bytes 2359300 | tf_op jit(solution)/shard_map/while
  347.0 9.8 %collective-permute-start.3 = (f32[4,192,128]{2,1,0:T(8,128)S(1)}, f32[4,192,128]{2,1,0:T(8,128)S(1)}, u32[]{:S(2)}, u32[]{:S(2)}) collective-permute-start(f32[4,192,128]{2,1,0:T(8,128)S(1)} %get-tuple-element.469), channel_id=1, source_target_pairs={{0,4},{4,8},{8,12},{12,16},{16,20},{20,24},{24,28},{28,32},{32,36}... | collective-permute-start | bytes 1179656 | tf_op jit(solution)/shard_map/while/body/eval_jaxpr/ppermute | solution.py:15
  351.9 11.4 %collective-permute-start.2 = (f32[4,192,128]{2,1,0:T(8,128)S(1)}, f32[4,192,128]{2,1,0:T(8,128)S(1)}, u32[]{:S(2)}, u32[]{:S(2)}) collective-permute-start(f32[4,192,128]{2,1,0:T(8,128)S(1)} %get-tuple-element.468), channel_id=1, source_target_pairs={{4,0},{8,4},{12,8},{16,12},{20,16},{24,20},{28,24},{32,28},{36,32}... | collective-permute-start | bytes 1179656 | tf_op jit(solution)/shard_map/while/body/eval_jaxpr/ppermute | solution.py:18
  375.0 20.0 %collective-permute-start.3 = (f32[4,192,128]{2,1,0:T(8,128)S(1)}, f32[4,192,128]{2,1,0:T(8,128)S(1)}, u32[]{:S(2)}, u32[]{:S(2)}) collective-permute-start(f32[4,192,128]{2,1,0:T(8,128)S(1)} %get-tuple-element.469), channel_id=1, source_target_pairs={{0,4},{4,8},{8,12},{12,16},{16,20},{20,24},{24,28},{28,32},{32,36}... | collective-permute-start | bytes 1179656 | tf_op jit(solution)/shard_map/while/body/eval_jaxpr/ppermute | solution.py:15
  380.4 20.0 %collective-permute-start.2 = (f32[4,192,128]{2,1,0:T(8,128)S(1)}, f32[4,192,128]{2,1,0:T(8,128)S(1)}, u32[]{:S(2)}, u32[]{:S(2)}) collective-permute-start(f32[4,192,128]{2,1,0:T(8,128)S(1)} %get-tuple-element.468), channel_id=1, source_target_pairs={{4,0},{8,4},{12,8},{16,12},{20,16},{24,20},{28,24},{32,28},{36,32}... | collective-permute-start | bytes 1179656 | tf_op jit(solution)/shard_map/while/body/eval_jaxpr/ppermute | solution.py:18
  412.1 10.6 %collective-permute-start.3 = (f32[4,192,128]{2,1,0:T(8,128)S(1)}, f32[4,192,128]{2,1,0:T(8,128)S(1)}, u32[]{:S(2)}, u32[]{:S(2)}) collective-permute-start(f32[4,192,128]{2,1,0:T(8,128)S(1)} %get-tuple-element.469), channel_id=1, source_target_pairs={{0,4},{4,8},{8,12},{12,16},{16,20},{20,24},{24,28},{28,32},{32,36}... | collective-permute-start | bytes 1179656 | tf_op jit(solution)/shard_map/while/body/eval_jaxpr/ppermute | solution.py:15
  417.3 16.0 %collective-permute-start.2 = (f32[4,192,128]{2,1,0:T(8,128)S(1)}, f32[4,192,128]{2,1,0:T(8,128)S(1)}, u32[]{:S(2)}, u32[]{:S(2)}) collective-permute-start(f32[4,192,128]{2,1,0:T(8,128)S(1)} %get-tuple-element.468), channel_id=1, source_target_pairs={{4,0},{8,4},{12,8},{16,12},{20,16},{24,20},{28,24},{32,28},{36,32}... | collective-permute-start | bytes 1179656 | tf_op jit(solution)/shard_map/while/body/eval_jaxpr/ppermute | solution.py:18
  422.9 11.5 %copy-start.3 = (f32[8,192,128]{2,1,0:T(8,128)S(1)}, f32[8,192,128]{2,1,0:T(8,128)}, u32[]{:S(2)}) copy-start(f32[8,192,128]{2,1,0:T(8,128)} %get-tuple-element.518) | copy-start | bytes 2359300 | tf_op jit(solution)/shard_map/while
  445.0 12.5 %collective-permute-start.3 = (f32[4,192,128]{2,1,0:T(8,128)S(1)}, f32[4,192,128]{2,1,0:T(8,128)S(1)}, u32[]{:S(2)}, u32[]{:S(2)}) collective-permute-start(f32[4,192,128]{2,1,0:T(8,128)S(1)} %get-tuple-element.469), channel_id=1, source_target_pairs={{0,4},{4,8},{8,12},{12,16},{16,20},{20,24},{24,28},{28,32},{32,36}... | collective-permute-start | bytes 1179656 | tf_op jit(solution)/shard_map/while/body/eval_jaxpr/ppermute | solution.py:15
  450.3 15.4 %collective-permute-start.2 = (f32[4,192,128]{2,1,0:T(8,128)S(1)}, f32[4,192,128]{2,1,0:T(8,128)S(1)}, u32[]{:S(2)}, u32[]{:S(2)}) collective-permute-start(f32[4,192,128]{2,1,0:T(8,128)S(1)} %get-tuple-element.468), channel_id=1, source_target_pairs={{4,0},{8,4},{12,8},{16,12},{20,16},{24,20},{28,24},{32,28},{36,32}... | collective-permute-start | bytes 1179656 | tf_op jit(solution)/shard_map/while/body/eval_jaxpr/ppermute | solution.py:18
  477.3 13.2 %collective-permute-start.3 = (f32[4,192,128]{2,1,0:T(8,128)S(1)}, f32[4,192,128]{2,1,0:T(8,128)S(1)}, u32[]{:S(2)}, u32[]{:S(2)}) collective-permute-start(f32[4,192,128]{2,1,0:T(8,128)S(1)} %get-tuple-element.469), channel_id=1, source_target_pairs={{0,4},{4,8},{8,12},{12,16},{16,20},{20,24},{24,28},{28,32},{32,36}... | collective-permute-start | bytes 1179656 | tf_op jit(solution)/shard_map/while/body/eval_jaxpr/ppermute | solution.py:15
  482.6 11.5 %collective-permute-start.2 = (f32[4,192,128]{2,1,0:T(8,128)S(1)}, f32[4,192,128]{2,1,0:T(8,128)S(1)}, u32[]{:S(2)}, u32[]{:S(2)}) collective-permute-start(f32[4,192,128]{2,1,0:T(8,128)S(1)} %get-tuple-element.468), channel_id=1, source_target_pairs={{4,0},{8,4},{12,8},{16,12},{20,16},{24,20},{28,24},{32,28},{36,32}... | collective-permute-start | bytes 1179656 | tf_op jit(solution)/shard_map/while/body/eval_jaxpr/ppermute | solution.py:18
  505.8 19.3 %collective-permute-start.3 = (f32[4,192,128]{2,1,0:T(8,128)S(1)}, f32[4,192,128]{2,1,0:T(8,128)S(1)}, u32[]{:S(2)}, u32[]{:S(2)}) collective-permute-start(f32[4,192,128]{2,1,0:T(8,128)S(1)} %get-tuple-element.469), channel_id=1, source_target_pairs={{0,4},{4,8},{8,12},{12,16},{16,20},{20,24},{24,28},{28,32},{32,36}... | collective-permute-start | bytes 1179656 | tf_op jit(solution)/shard_map/while/body/eval_jaxpr/ppermute | solution.py:15
  510.5 20.2 %collective-permute-start.2 = (f32[4,192,128]{2,1,0:T(8,128)S(1)}, f32[4,192,128]{2,1,0:T(8,128)S(1)}, u32[]{:S(2)}, u32[]{:S(2)}) collective-permute-start(f32[4,192,128]{2,1,0:T(8,128)S(1)} %get-tuple-element.468), channel_id=1, source_target_pairs={{4,0},{8,4},{12,8},{16,12},{20,16},{24,20},{28,24},{32,28},{36,32}... | collective-permute-start | bytes 1179656 | tf_op jit(solution)/shard_map/while/body/eval_jaxpr/ppermute | solution.py:18
  542.4 10.4 %collective-permute-start.3 = (f32[4,192,128]{2,1,0:T(8,128)S(1)}, f32[4,192,128]{2,1,0:T(8,128)S(1)}, u32[]{:S(2)}, u32[]{:S(2)}) collective-permute-start(f32[4,192,128]{2,1,0:T(8,128)S(1)} %get-tuple-element.469), channel_id=1, source_target_pairs={{0,4},{4,8},{8,12},{12,16},{16,20},{20,24},{24,28},{28,32},{32,36}... | collective-permute-start | bytes 1179656 | tf_op jit(solution)/shard_map/while/body/eval_jaxpr/ppermute | solution.py:15
  547.3 16.4 %collective-permute-start.2 = (f32[4,192,128]{2,1,0:T(8,128)S(1)}, f32[4,192,128]{2,1,0:T(8,128)S(1)}, u32[]{:S(2)}, u32[]{:S(2)}) collective-permute-start(f32[4,192,128]{2,1,0:T(8,128)S(1)} %get-tuple-element.468), channel_id=1, source_target_pairs={{4,0},{8,4},{12,8},{16,12},{20,16},{24,20},{28,24},{32,28},{36,32}... | collective-permute-start | bytes 1179656 | tf_op jit(solution)/shard_map/while/body/eval_jaxpr/ppermute | solution.py:18
  553.0 11.7 %copy-start.3 = (f32[8,192,128]{2,1,0:T(8,128)S(1)}, f32[8,192,128]{2,1,0:T(8,128)}, u32[]{:S(2)}) copy-start(f32[8,192,128]{2,1,0:T(8,128)} %get-tuple-element.518) | copy-start | bytes 2359300 | tf_op jit(solution)/shard_map/while
  575.4 12.3 %collective-permute-start.3 = (f32[4,192,128]{2,1,0:T(8,128)S(1)}, f32[4,192,128]{2,1,0:T(8,128)S(1)}, u32[]{:S(2)}, u32[]{:S(2)}) collective-permute-start(f32[4,192,128]{2,1,0:T(8,128)S(1)} %get-tuple-element.469), channel_id=1, source_target_pairs={{0,4},{4,8},{8,12},{12,16},{16,20},{20,24},{24,28},{28,32},{32,36}... | collective-permute-start | bytes 1179656 | tf_op jit(solution)/shard_map/while/body/eval_jaxpr/ppermute | solution.py:15
  580.3 15.4 %collective-permute-start.2 = (f32[4,192,128]{2,1,0:T(8,128)S(1)}, f32[4,192,128]{2,1,0:T(8,128)S(1)}, u32[]{:S(2)}, u32[]{:S(2)}) collective-permute-start(f32[4,192,128]{2,1,0:T(8,128)S(1)} %get-tuple-element.468), channel_id=1, source_target_pairs={{4,0},{8,4},{12,8},{16,12},{20,16},{24,20},{28,24},{32,28},{36,32}... | collective-permute-start | bytes 1179656 | tf_op jit(solution)/shard_map/while/body/eval_jaxpr/ppermute | solution.py:18
  607.4 13.2 %collective-permute-start.3 = (f32[4,192,128]{2,1,0:T(8,128)S(1)}, f32[4,192,128]{2,1,0:T(8,128)S(1)}, u32[]{:S(2)}, u32[]{:S(2)}) collective-permute-start(f32[4,192,128]{2,1,0:T(8,128)S(1)} %get-tuple-element.469), channel_id=1, source_target_pairs={{0,4},{4,8},{8,12},{12,16},{16,20},{20,24},{24,28},{28,32},{32,36}... | collective-permute-start | bytes 1179656 | tf_op jit(solution)/shard_map/while/body/eval_jaxpr/ppermute | solution.py:15
  612.7 11.5 %collective-permute-start.2 = (f32[4,192,128]{2,1,0:T(8,128)S(1)}, f32[4,192,128]{2,1,0:T(8,128)S(1)}, u32[]{:S(2)}, u32[]{:S(2)}) collective-permute-start(f32[4,192,128]{2,1,0:T(8,128)S(1)} %get-tuple-element.468), channel_id=1, source_target_pairs={{4,0},{8,4},{12,8},{16,12},{20,16},{24,20},{28,24},{32,28},{36,32}... | collective-permute-start | bytes 1179656 | tf_op jit(solution)/shard_map/while/body/eval_jaxpr/ppermute | solution.py:18
  635.9 19.3 %collective-permute-start.3 = (f32[4,192,128]{2,1,0:T(8,128)S(1)}, f32[4,192,128]{2,1,0:T(8,128)S(1)}, u32[]{:S(2)}, u32[]{:S(2)}) collective-permute-start(f32[4,192,128]{2,1,0:T(8,128)S(1)} %get-tuple-element.469), channel_id=1, source_target_pairs={{0,4},{4,8},{8,12},{12,16},{16,20},{20,24},{24,28},{28,32},{32,36}... | collective-permute-start | bytes 1179656 | tf_op jit(solution)/shard_map/while/body/eval_jaxpr/ppermute | solution.py:15
  640.6 20.2 %collective-permute-start.2 = (f32[4,192,128]{2,1,0:T(8,128)S(1)}, f32[4,192,128]{2,1,0:T(8,128)S(1)}, u32[]{:S(2)}, u32[]{:S(2)}) collective-permute-start(f32[4,192,128]{2,1,0:T(8,128)S(1)} %get-tuple-element.468), channel_id=1, source_target_pairs={{4,0},{8,4},{12,8},{16,12},{20,16},{24,20},{28,24},{32,28},{36,32}... | collective-permute-start | bytes 1179656 | tf_op jit(solution)/shard_map/while/body/eval_jaxpr/ppermute | solution.py:18
  (50 other events, 216.6 us)
Sparse Core Ops, SparseCore 0:
  672.6 91.8 all-reduce.3
where the time goes:
time: 777 us; the launch traced here: 773 us
  waiting for transfers between devices  349 us (45%)
  other arithmetic  199 us (26%)
  starting transfers between devices  110 us (14%)
  local copies, waits for them, and re-layouts  97.8 us (13%)
  between operations  14.1 us (2%)
    ppermute x20, waiting for transfers between devices, with_halo(): lax.ppermute(lax.slice_in_dim(block, 0, width, axis=dim), axis, backward)  164 us
    ppermute x20, waiting for transfers between devices, with_halo(): lax.ppermute(lax.slice_in_dim(block, block.shape[dim] - width, None, axis...  93.7 us
    psum x1, waiting for transfers between devices, per_device(): summed = lax.psum(imaging, 'shot')  92 us
    ppermute x20, starting transfers between devices, with_halo(): lax.ppermute(lax.slice_in_dim(block, block.shape[dim] - width, None, axis...  84.2 us
    scatter-add x10, other arithmetic, backward(): earlier.reshape(-1).at[receiver_cells].add(residual).reshape(velocity.shape)  37.4 us
    add x10, other arithmetic, backward(): 2.0 * following - furthest + courant_sq * laplace(edge_layers(following))  32.8 us
    add x10, other arithmetic, forward(): latest = 2.0 * current - former + courant_sq * laplace(edge_layers(current))  32.8 us
    while x180, local copies, waits for them, and re-layouts  32.6 us
  transfers between devices with their start and end apart: 41, of which 41 were waited for; matrix products, arithmetic and copies ran while one was open for 4% of the time, Pallas kernels for 0%

commit v1 on v0

--- a/solution.py
+++ b/solution.py
@@ -108,7 +108,7 @@
     band_rows = extent_y // lax.axis_size("shot")
     offset = lax.axis_index("shot") * band_rows
     factor = lax.dynamic_slice_in_dim(-2.0 / velocity**3, offset, band_rows, 1)
-    summed = lax.psum(imaging, "shot")
+    summed = jnp.sum(lax.all_gather(imaging, "shot"), axis=0)
     own_band = lax.dynamic_slice_in_dim(summed, offset, band_rows, 1)
     return factor * own_band
 

time: 777 us -> 760 us (0.978)
  waiting for transfers between devices: 349 us -> 330 us
    psum x1 -> x0, waiting for transfers between devices: 92 us -> none  [per_device(): summed = lax.psum(imaging, 'shot')]
    all_gather x0 -> x1, waiting for transfers between devices: none -> 73 us  [per_device(): summed = jnp.sum(lax.all_gather(imaging, 'shot'), axis=0)]
where the time goes in v1:
time: 760 us; the launch traced here: 756 us
  waiting for transfers between devices  330 us (43%)
  other arithmetic  202 us (27%)
  starting transfers between devices  110 us (14%)
  local copies, waits for them, and re-layouts  97.8 us (13%)
  between operations  14.1 us (2%)
    ppermute x20, waiting for transfers between devices, with_halo(): lax.ppermute(lax.slice_in_dim(block, 0, width, axis=dim), axis, backward)  164 us
    ppermute x20, waiting for transfers between devices, with_halo(): lax.ppermute(lax.slice_in_dim(block, block.shape[dim] - width, None, axis...  93.7 us
    ppermute x20, starting transfers between devices, with_halo(): lax.ppermute(lax.slice_in_dim(block, block.shape[dim] - width, None, axis...  84.2 us
    all_gather x1, waiting for transfers between devices, per_device(): summed = jnp.sum(lax.all_gather(imaging, 'shot'), axis=0)  73 us
    scatter-add x10, other arithmetic, backward(): earlier.reshape(-1).at[receiver_cells].add(residual).reshape(velocity.shape)  37.4 us
    add x10, other arithmetic, backward(): 2.0 * following - furthest + courant_sq * laplace(edge_layers(following))  32.8 us
    add x10, other arithmetic, forward(): latest = 2.0 * current - former + courant_sq * laplace(edge_layers(current))  32.8 us
    while x180, local copies, waits for them, and re-layouts  32.6 us
  transfers between devices with their start and end apart: 41, of which 41 were waited for; matrix products, arithmetic and copies ran while one was open for 4% of the time, Pallas kernels for 0%

profile of v1, /device:TPU:1, one launch (start us, length us, event | category | flops | bytes accessed | tf_op | source)
XLA Modules:
  0.0 756.1 jit_solution(16264275625847629511)
XLA Ops:
  12.2 333.3 %while.37 = (s32[]{:T(128)}, f32[8,192,128]{2,1,0:T(8,128)S(1)}, f32[8,192,128]{2,1,0:T(8,128)}, f32[10,8,192,128]{3,2,1,0:T(8,128)}, f32[10,512]{1,0:T(8,128)},...) while((s32[]{:T(128)}, f32[8,192,128]{2,1,0:T(8,128)S(1)}, ...), condition=%wide.region_2.3_spmd, body=%wide.region_0.2_spmd.sunk | while | flops 13609986 | bytes 43449096 | solution.py:88
  13.0 4.0 collective-permute-start.1
  22.2 13.2 %collective-permute-done = f32[4,192,128]{2,1,0:T(8,128)S(1)} collective-permute-done((f32[4,192,128]{2,1,0:T(8,128)S(1)}, f32[4,192,128]{2,1,0:T(8,128)S(1)}, u32[]{:S(2)}, u32[]{:S(2)}) %collective-permute-start) | collective-permute-done | bytes 393248 | tf_op jit(solution)/shard_map/while/body/eval_jaxpr/ppermute | solution.py:18
  56.1 4.0 collective-permute-done.1
  60.3 10.1 %collective-permute-done = f32[4,192,128]{2,1,0:T(8,128)S(1)} collective-permute-done((f32[4,192,128]{2,1,0:T(8,128)S(1)}, f32[4,192,128]{2,1,0:T(8,128)S(1)}, u32[]{:S(2)}, u32[]{:S(2)}) %collective-permute-start) | collective-permute-done | bytes 393248 | tf_op jit(solution)/shard_map/while/body/eval_jaxpr/ppermute | solution.py:18
  94.5 9.8 %collective-permute-done = f32[4,192,128]{2,1,0:T(8,128)S(1)} collective-permute-done((f32[4,192,128]{2,1,0:T(8,128)S(1)}, f32[4,192,128]{2,1,0:T(8,128)S(1)}, u32[]{:S(2)}, u32[]{:S(2)}) %collective-permute-start) | collective-permute-done | bytes 393248 | tf_op jit(solution)/shard_map/while/body/eval_jaxpr/ppermute | solution.py:18
  127.4 9.7 %collective-permute-done = f32[4,192,128]{2,1,0:T(8,128)S(1)} collective-permute-done((f32[4,192,128]{2,1,0:T(8,128)S(1)}, f32[4,192,128]{2,1,0:T(8,128)S(1)}, u32[]{:S(2)}, u32[]{:S(2)}) %collective-permute-start) | collective-permute-done | bytes 393248 | tf_op jit(solution)/shard_map/while/body/eval_jaxpr/ppermute | solution.py:18
  159.2 8.4 %collective-permute-done = f32[4,192,128]{2,1,0:T(8,128)S(1)} collective-permute-done((f32[4,192,128]{2,1,0:T(8,128)S(1)}, f32[4,192,128]{2,1,0:T(8,128)S(1)}, u32[]{:S(2)}, u32[]{:S(2)}) %collective-permute-start) | collective-permute-done | bytes 393248 | tf_op jit(solution)/shard_map/while/body/eval_jaxpr/ppermute | solution.py:18
  190.1 8.0 %collective-permute-done = f32[4,192,128]{2,1,0:T(8,128)S(1)} collective-permute-done((f32[4,192,128]{2,1,0:T(8,128)S(1)}, f32[4,192,128]{2,1,0:T(8,128)S(1)}, u32[]{:S(2)}, u32[]{:S(2)}) %collective-permute-start) | collective-permute-done | bytes 393248 | tf_op jit(solution)/shard_map/while/body/eval_jaxpr/ppermute | solution.py:18
  219.2 5.9 collective-permute-done
  245.8 4.1 collective-permute-done.1
  250.1 10.8 %collective-permute-done = f32[4,192,128]{2,1,0:T(8,128)S(1)} collective-permute-done((f32[4,192,128]{2,1,0:T(8,128)S(1)}, f32[4,192,128]{2,1,0:T(8,128)S(1)}, u32[]{:S(2)}, u32[]{:S(2)}) %collective-permute-start) | collective-permute-done | bytes 393248 | tf_op jit(solution)/shard_map/while/body/eval_jaxpr/ppermute | solution.py:18
  275.3 5.2 collective-permute-start.1
  285.8 11.1 %collective-permute-done = f32[4,192,128]{2,1,0:T(8,128)S(1)} collective-permute-done((f32[4,192,128]{2,1,0:T(8,128)S(1)}, f32[4,192,128]{2,1,0:T(8,128)S(1)}, u32[]{:S(2)}, u32[]{:S(2)}) %collective-permute-start) | collective-permute-done | bytes 393248 | tf_op jit(solution)/shard_map/while/body/eval_jaxpr/ppermute | solution.py:18
  311.3 5.2 collective-permute-start.1
  321.8 10.1 %collective-permute-done = f32[4,192,128]{2,1,0:T(8,128)S(1)} collective-permute-done((f32[4,192,128]{2,1,0:T(8,128)S(1)}, f32[4,192,128]{2,1,0:T(8,128)S(1)}, u32[]{:S(2)}, u32[]{:S(2)}) %collective-permute-start) | collective-permute-done | bytes 393248 | tf_op jit(solution)/shard_map/while/body/eval_jaxpr/ppermute | solution.py:18
  346.9 325.5 %while.38 = (s32[]{:T(128)}, f32[8,192,128]{2,1,0:T(8,128)S(1)}, f32[8,192,128]{2,1,0:T(8,128)}, f32[8,192,128]{2,1,0:T(8,128)}, f32[8,192,128]{2,1,0:T(8,128)S(...) while((s32[]{:T(128)}, f32[8,192,128]{2,1,0:T(8,128)S(1)}, ...), condition=%wide.region_5.6_spmd.clone, body=%wide.region_3.5_spmd.clone.sunk | while | flops 13607940 | bytes 49729836 | solution.py:102
  347.0 4.9 collective-permute-start.3
  357.0 6.4 collective-permute-done.2
  375.0 5.3 collective-permute-start.3
  382.4 12.6 %collective-permute-done.3 = f32[4,192,128]{2,1,0:T(8,128)S(1)} collective-permute-done((f32[4,192,128]{2,1,0:T(8,128)S(1)}, f32[4,192,128]{2,1,0:T(8,128)S(1)}, u32[]{:S(2)}, u32[]{:S(2)}) %collective-permute-start.3) | collective-permute-done | bytes 393248 | tf_op jit(solution)/shard_map/while/body/eval_jaxpr/ppermute | solution.py:15
  395.2 5.2 collective-permute-done.2
  412.1 5.3 collective-permute-start.3
  422.9 10.5 %collective-permute-done.2 = f32[4,192,128]{2,1,0:T(8,128)S(1)} collective-permute-done((f32[4,192,128]{2,1,0:T(8,128)S(1)}, f32[4,192,128]{2,1,0:T(8,128)S(1)}, u32[]{:S(2)}, u32[]{:S(2)}) %collective-permute-start.2) | collective-permute-done | bytes 393248 | tf_op jit(solution)/shard_map/while/body/eval_jaxpr/ppermute | solution.py:18
  445.0 5.2 collective-permute-start.3
  452.3 5.2 collective-permute-done.3
  457.7 7.9 %collective-permute-done.2 = f32[4,192,128]{2,1,0:T(8,128)S(1)} collective-permute-done((f32[4,192,128]{2,1,0:T(8,128)S(1)}, f32[4,192,128]{2,1,0:T(8,128)S(1)}, u32[]{:S(2)}, u32[]{:S(2)}) %collective-permute-start.2) | collective-permute-done | bytes 393248 | tf_op jit(solution)/shard_map/while/body/eval_jaxpr/ppermute | solution.py:18
  470.8 3.7 scatter_fusion.1
  477.3 5.3 collective-permute-start.3
  484.7 5.9 collective-permute-done.3
  505.8 4.7 collective-permute-start.3
  512.5 12.5 %collective-permute-done.3 = f32[4,192,128]{2,1,0:T(8,128)S(1)} collective-permute-done((f32[4,192,128]{2,1,0:T(8,128)S(1)}, f32[4,192,128]{2,1,0:T(8,128)S(1)}, u32[]{:S(2)}, u32[]{:S(2)}) %collective-permute-start.3) | collective-permute-done | bytes 393248 | tf_op jit(solution)/shard_map/while/body/eval_jaxpr/ppermute | solution.py:15
  525.3 5.4 collective-permute-done.2
  535.9 3.7 scatter_fusion.1
  542.4 5.0 collective-permute-start.3
  553.0 10.7 %collective-permute-done.2 = f32[4,192,128]{2,1,0:T(8,128)S(1)} collective-permute-done((f32[4,192,128]{2,1,0:T(8,128)S(1)}, f32[4,192,128]{2,1,0:T(8,128)S(1)}, u32[]{:S(2)}, u32[]{:S(2)}) %collective-permute-start.2) | collective-permute-done | bytes 393248 | tf_op jit(solution)/shard_map/while/body/eval_jaxpr/ppermute | solution.py:18
  568.9 3.7 scatter_fusion.1
  575.4 5.0 collective-permute-start.3
  582.4 5.3 collective-permute-done.3
  587.8 7.9 %collective-permute-done.2 = f32[4,192,128]{2,1,0:T(8,128)S(1)} collective-permute-done((f32[4,192,128]{2,1,0:T(8,128)S(1)}, f32[4,192,128]{2,1,0:T(8,128)S(1)}, u32[]{:S(2)}, u32[]{:S(2)}) %collective-permute-start.2) | collective-permute-done | bytes 393248 | tf_op jit(solution)/shard_map/while/body/eval_jaxpr/ppermute | solution.py:18
  601.0 3.7 scatter_fusion.1
  607.4 5.3 collective-permute-start.3
  614.8 5.9 collective-permute-done.3
  635.9 4.7 collective-permute-start.3
  642.6 12.6 %collective-permute-done.3 = f32[4,192,128]{2,1,0:T(8,128)S(1)} collective-permute-done((f32[4,192,128]{2,1,0:T(8,128)S(1)}, f32[4,192,128]{2,1,0:T(8,128)S(1)}, u32[]{:S(2)}, u32[]{:S(2)}) %collective-permute-start.3) | collective-permute-done | bytes 393248 | tf_op jit(solution)/shard_map/while/body/eval_jaxpr/ppermute | solution.py:15
  655.4 5.4 collective-permute-done.2
  666.0 3.7 scatter_fusion.1
  672.5 73.0 %all-gather.3.cloned.1.call-done = f32[32,192,128]{2,1,0:T(8,128)} async-done(((f32[8,192,128]{2,1,0:T(8,128)}), f32[32,192,128]{2,1,0:T(8,128)}) %all-gather.3.cloned.1.call-update) | async-done | bytes 3145744 | tf_op jit(solution)/shard_map/all_gather | solution.py:111
  (443 shorter events, 358.2 us)
Async XLA Ops:
  6.5 738.9 %all-gather.3.cloned.1.call-start = ((), (), s32[]{:S(2)}) async-start(), calls=%async_computation | async-start | bytes 3932160 | tf_op jit(solution)/shard_map/all_gather | solution.py:111
  12.2 334.7 %copy-start.1 = (f32[1,8,192,128]{3,2,1,0:T(8,128)S(1)}, f32[1,8,192,128]{3,2,1,0:T(8,128)}, u32[]{:S(2)}) copy-start(f32[1,8,192,128]{3,2,1,0:T(8,128)} %param.17) | copy-start | bytes 2359300
  13.0 9.0 %collective-permute-start.1 = (f32[4,192,128]{2,1,0:T(8,128)}, f32[4,192,128]{2,1,0:T(8,128)S(1)}, u32[]{:S(2)}, u32[]{:S(2)}) collective-permute-start(f32[4,192,128]{2,1,0:T(8,128)} %get-tuple-element.457), channel_id=1, source_target_pairs={{0,4},{4,8},{8,12},{12,16},{16,20},{20,24},{24,28},{28,32},{32,36}... | collective-permute-start | bytes 1179656 | tf_op jit(solution)/shard_map/while/body/eval_jaxpr/ppermute | solution.py:15
  17.0 18.4 %collective-permute-start = (f32[4,192,128]{2,1,0:T(8,128)S(1)}, f32[4,192,128]{2,1,0:T(8,128)S(1)}, u32[]{:S(2)}, u32[]{:S(2)}) collective-permute-start(f32[4,192,128]{2,1,0:T(8,128)S(1)} %get-tuple-element.456), channel_id=1, source_target_pairs={{4,0},{8,4},{12,8},{16,12},{20,16},{24,20},{28,24},{32,28},{36,32}... | collective-permute-start | bytes 1179656 | tf_op jit(solution)/shard_map/while/body/eval_jaxpr/ppermute | solution.py:18
  22.2 14.2 %copy-start.2 = (f32[8,192,128]{2,1,0:T(8,128)S(1)}, f32[8,192,128]{2,1,0:T(8,128)}, u32[]{:S(2)}) copy-start(f32[8,192,128]{2,1,0:T(8,128)} %get-tuple-element.485) | copy-start | bytes 2359300 | tf_op jit(solution)/shard_map/while
  49.9 10.3 %collective-permute-start.1 = (f32[4,192,128]{2,1,0:T(8,128)}, f32[4,192,128]{2,1,0:T(8,128)S(1)}, u32[]{:S(2)}, u32[]{:S(2)}) collective-permute-start(f32[4,192,128]{2,1,0:T(8,128)} %get-tuple-element.457), channel_id=1, source_target_pairs={{0,4},{4,8},{8,12},{12,16},{16,20},{20,24},{24,28},{28,32},{32,36}... | collective-permute-start | bytes 1179656 | tf_op jit(solution)/shard_map/while/body/eval_jaxpr/ppermute | solution.py:15
  53.0 17.5 %collective-permute-start = (f32[4,192,128]{2,1,0:T(8,128)S(1)}, f32[4,192,128]{2,1,0:T(8,128)S(1)}, u32[]{:S(2)}, u32[]{:S(2)}) collective-permute-start(f32[4,192,128]{2,1,0:T(8,128)S(1)} %get-tuple-element.456), channel_id=1, source_target_pairs={{4,0},{8,4},{12,8},{16,12},{20,16},{24,20},{28,24},{32,28},{36,32}... | collective-permute-start | bytes 1179656 | tf_op jit(solution)/shard_map/while/body/eval_jaxpr/ppermute | solution.py:18
  84.9 9.3 %collective-permute-start.1 = (f32[4,192,128]{2,1,0:T(8,128)}, f32[4,192,128]{2,1,0:T(8,128)S(1)}, u32[]{:S(2)}, u32[]{:S(2)}) collective-permute-start(f32[4,192,128]{2,1,0:T(8,128)} %get-tuple-element.457), channel_id=1, source_target_pairs={{0,4},{4,8},{8,12},{12,16},{16,20},{20,24},{24,28},{28,32},{32,36}... | collective-permute-start | bytes 1179656 | tf_op jit(solution)/shard_map/while/body/eval_jaxpr/ppermute | solution.py:15
  88.1 16.2 %collective-permute-start = (f32[4,192,128]{2,1,0:T(8,128)S(1)}, f32[4,192,128]{2,1,0:T(8,128)S(1)}, u32[]{:S(2)}, u32[]{:S(2)}) collective-permute-start(f32[4,192,128]{2,1,0:T(8,128)S(1)} %get-tuple-element.456), channel_id=1, source_target_pairs={{4,0},{8,4},{12,8},{16,12},{20,16},{24,20},{28,24},{32,28},{36,32}... | collective-permute-start | bytes 1179656 | tf_op jit(solution)/shard_map/while/body/eval_jaxpr/ppermute | solution.py:18
  118.8 8.4 %collective-permute-start.1 = (f32[4,192,128]{2,1,0:T(8,128)}, f32[4,192,128]{2,1,0:T(8,128)S(1)}, u32[]{:S(2)}, u32[]{:S(2)}) collective-permute-start(f32[4,192,128]{2,1,0:T(8,128)} %get-tuple-element.457), channel_id=1, source_target_pairs={{0,4},{4,8},{8,12},{12,16},{16,20},{20,24},{24,28},{28,32},{32,36}... | collective-permute-start | bytes 1179656 | tf_op jit(solution)/shard_map/while/body/eval_jaxpr/ppermute | solution.py:15
  121.9 15.2 %collective-permute-start = (f32[4,192,128]{2,1,0:T(8,128)S(1)}, f32[4,192,128]{2,1,0:T(8,128)S(1)}, u32[]{:S(2)}, u32[]{:S(2)}) collective-permute-start(f32[4,192,128]{2,1,0:T(8,128)S(1)} %get-tuple-element.456), channel_id=1, source_target_pairs={{4,0},{8,4},{12,8},{16,12},{20,16},{24,20},{28,24},{32,28},{36,32}... | collective-permute-start | bytes 1179656 | tf_op jit(solution)/shard_map/while/body/eval_jaxpr/ppermute | solution.py:18
  151.5 7.5 collective-permute-start.1
  154.0 13.6 %collective-permute-start = (f32[4,192,128]{2,1,0:T(8,128)S(1)}, f32[4,192,128]{2,1,0:T(8,128)S(1)}, u32[]{:S(2)}, u32[]{:S(2)}) collective-permute-start(f32[4,192,128]{2,1,0:T(8,128)S(1)} %get-tuple-element.456), channel_id=1, source_target_pairs={{4,0},{8,4},{12,8},{16,12},{20,16},{24,20},{28,24},{32,28},{36,32}... | collective-permute-start | bytes 1179656 | tf_op jit(solution)/shard_map/while/body/eval_jaxpr/ppermute | solution.py:18
  182.1 7.8 %collective-permute-start.1 = (f32[4,192,128]{2,1,0:T(8,128)}, f32[4,192,128]{2,1,0:T(8,128)S(1)}, u32[]{:S(2)}, u32[]{:S(2)}) collective-permute-start(f32[4,192,128]{2,1,0:T(8,128)} %get-tuple-element.457), channel_id=1, source_target_pairs={{0,4},{4,8},{8,12},{12,16},{16,20},{20,24},{24,28},{28,32},{32,36}... | collective-permute-start | bytes 1179656 | tf_op jit(solution)/shard_map/while/body/eval_jaxpr/ppermute | solution.py:15
  184.9 13.2 %collective-permute-start = (f32[4,192,128]{2,1,0:T(8,128)S(1)}, f32[4,192,128]{2,1,0:T(8,128)S(1)}, u32[]{:S(2)}, u32[]{:S(2)}) collective-permute-start(f32[4,192,128]{2,1,0:T(8,128)S(1)} %get-tuple-element.456), channel_id=1, source_target_pairs={{4,0},{8,4},{12,8},{16,12},{20,16},{24,20},{28,24},{32,28},{36,32}... | collective-permute-start | bytes 1179656 | tf_op jit(solution)/shard_map/while/body/eval_jaxpr/ppermute | solution.py:18
  212.5 6.5 collective-permute-start.1
  214.0 11.1 %collective-permute-start = (f32[4,192,128]{2,1,0:T(8,128)S(1)}, f32[4,192,128]{2,1,0:T(8,128)S(1)}, u32[]{:S(2)}, u32[]{:S(2)}) collective-permute-start(f32[4,192,128]{2,1,0:T(8,128)S(1)} %get-tuple-element.456), channel_id=1, source_target_pairs={{4,0},{8,4},{12,8},{16,12},{20,16},{24,20},{28,24},{32,28},{36,32}... | collective-permute-start | bytes 1179656 | tf_op jit(solution)/shard_map/while/body/eval_jaxpr/ppermute | solution.py:18
  239.6 10.3 %collective-permute-start.1 = (f32[4,192,128]{2,1,0:T(8,128)}, f32[4,192,128]{2,1,0:T(8,128)S(1)}, u32[]{:S(2)}, u32[]{:S(2)}) collective-permute-start(f32[4,192,128]{2,1,0:T(8,128)} %get-tuple-element.457), channel_id=1, source_target_pairs={{0,4},{4,8},{8,12},{12,16},{16,20},{20,24},{24,28},{28,32},{32,36}... | collective-permute-start | bytes 1179656 | tf_op jit(solution)/shard_map/while/body/eval_jaxpr/ppermute | solution.py:15
  242.6 18.3 %collective-permute-start = (f32[4,192,128]{2,1,0:T(8,128)S(1)}, f32[4,192,128]{2,1,0:T(8,128)S(1)}, u32[]{:S(2)}, u32[]{:S(2)}) collective-permute-start(f32[4,192,128]{2,1,0:T(8,128)S(1)} %get-tuple-element.456), channel_id=1, source_target_pairs={{4,0},{8,4},{12,8},{16,12},{20,16},{24,20},{28,24},{32,28},{36,32}... | collective-permute-start | bytes 1179656 | tf_op jit(solution)/shard_map/while/body/eval_jaxpr/ppermute | solution.py:18
  250.0 11.8 %copy-start.2 = (f32[8,192,128]{2,1,0:T(8,128)S(1)}, f32[8,192,128]{2,1,0:T(8,128)}, u32[]{:S(2)}) copy-start(f32[8,192,128]{2,1,0:T(8,128)} %get-tuple-element.485) | copy-start | bytes 2359300 | tf_op jit(solution)/shard_map/while
  275.3 10.2 %collective-permute-start.1 = (f32[4,192,128]{2,1,0:T(8,128)}, f32[4,192,128]{2,1,0:T(8,128)S(1)}, u32[]{:S(2)}, u32[]{:S(2)}) collective-permute-start(f32[4,192,128]{2,1,0:T(8,128)} %get-tuple-element.457), channel_id=1, source_target_pairs={{0,4},{4,8},{8,12},{12,16},{16,20},{20,24},{24,28},{28,32},{32,36}... | collective-permute-start | bytes 1179656 | tf_op jit(solution)/shard_map/while/body/eval_jaxpr/ppermute | solution.py:15
  280.6 16.3 %collective-permute-start = (f32[4,192,128]{2,1,0:T(8,128)S(1)}, f32[4,192,128]{2,1,0:T(8,128)S(1)}, u32[]{:S(2)}, u32[]{:S(2)}) collective-permute-start(f32[4,192,128]{2,1,0:T(8,128)S(1)} %get-tuple-element.456), channel_id=1, source_target_pairs={{4,0},{8,4},{12,8},{16,12},{20,16},{24,20},{28,24},{32,28},{36,32}... | collective-permute-start | bytes 1179656 | tf_op jit(solution)/shard_map/while/body/eval_jaxpr/ppermute | solution.py:18
  285.8 12.0 %copy-start.2 = (f32[8,192,128]{2,1,0:T(8,128)S(1)}, f32[8,192,128]{2,1,0:T(8,128)}, u32[]{:S(2)}) copy-start(f32[8,192,128]{2,1,0:T(8,128)} %get-tuple-element.485) | copy-start | bytes 2359300 | tf_op jit(solution)/shard_map/while
  311.3 10.2 %collective-permute-start.1 = (f32[4,192,128]{2,1,0:T(8,128)}, f32[4,192,128]{2,1,0:T(8,128)S(1)}, u32[]{:S(2)}, u32[]{:S(2)}) collective-permute-start(f32[4,192,128]{2,1,0:T(8,128)} %get-tuple-element.457), channel_id=1, source_target_pairs={{0,4},{4,8},{8,12},{12,16},{16,20},{20,24},{24,28},{28,32},{32,36}... | collective-permute-start | bytes 1179656 | tf_op jit(solution)/shard_map/while/body/eval_jaxpr/ppermute | solution.py:15
  316.6 15.3 %collective-permute-start = (f32[4,192,128]{2,1,0:T(8,128)S(1)}, f32[4,192,128]{2,1,0:T(8,128)S(1)}, u32[]{:S(2)}, u32[]{:S(2)}) collective-permute-start(f32[4,192,128]{2,1,0:T(8,128)S(1)} %get-tuple-element.456), channel_id=1, source_target_pairs={{4,0},{8,4},{12,8},{16,12},{20,16},{24,20},{28,24},{32,28},{36,32}... | collective-permute-start | bytes 1179656 | tf_op jit(solution)/shard_map/while/body/eval_jaxpr/ppermute | solution.py:18
  321.8 11.1 %copy-start.2 = (f32[8,192,128]{2,1,0:T(8,128)S(1)}, f32[8,192,128]{2,1,0:T(8,128)}, u32[]{:S(2)}) copy-start(f32[8,192,128]{2,1,0:T(8,128)} %get-tuple-element.485) | copy-start | bytes 2359300 | tf_op jit(solution)/shard_map/while
  347.0 9.8 %collective-permute-start.3 = (f32[4,192,128]{2,1,0:T(8,128)S(1)}, f32[4,192,128]{2,1,0:T(8,128)S(1)}, u32[]{:S(2)}, u32[]{:S(2)}) collective-permute-start(f32[4,192,128]{2,1,0:T(8,128)S(1)} %get-tuple-element.469), channel_id=1, source_target_pairs={{0,4},{4,8},{8,12},{12,16},{16,20},{20,24},{24,28},{28,32},{32,36}... | collective-permute-start | bytes 1179656 | tf_op jit(solution)/shard_map/while/body/eval_jaxpr/ppermute | solution.py:15
  351.9 11.4 %collective-permute-start.2 = (f32[4,192,128]{2,1,0:T(8,128)S(1)}, f32[4,192,128]{2,1,0:T(8,128)S(1)}, u32[]{:S(2)}, u32[]{:S(2)}) collective-permute-start(f32[4,192,128]{2,1,0:T(8,128)S(1)} %get-tuple-element.468), channel_id=1, source_target_pairs={{4,0},{8,4},{12,8},{16,12},{20,16},{24,20},{28,24},{32,28},{36,32}... | collective-permute-start | bytes 1179656 | tf_op jit(solution)/shard_map/while/body/eval_jaxpr/ppermute | solution.py:18
  375.0 20.0 %collective-permute-start.3 = (f32[4,192,128]{2,1,0:T(8,128)S(1)}, f32[4,192,128]{2,1,0:T(8,128)S(1)}, u32[]{:S(2)}, u32[]{:S(2)}) collective-permute-start(f32[4,192,128]{2,1,0:T(8,128)S(1)} %get-tuple-element.469), channel_id=1, source_target_pairs={{0,4},{4,8},{8,12},{12,16},{16,20},{20,24},{24,28},{28,32},{32,36}... | collective-permute-start | bytes 1179656 | tf_op jit(solution)/shard_map/while/body/eval_jaxpr/ppermute | solution.py:15
  380.4 20.0 %collective-permute-start.2 = (f32[4,192,128]{2,1,0:T(8,128)S(1)}, f32[4,192,128]{2,1,0:T(8,128)S(1)}, u32[]{:S(2)}, u32[]{:S(2)}) collective-permute-start(f32[4,192,128]{2,1,0:T(8,128)S(1)} %get-tuple-element.468), channel_id=1, source_target_pairs={{4,0},{8,4},{12,8},{16,12},{20,16},{24,20},{28,24},{32,28},{36,32}... | collective-permute-start | bytes 1179656 | tf_op jit(solution)/shard_map/while/body/eval_jaxpr/ppermute | solution.py:18
  412.1 10.6 %collective-permute-start.3 = (f32[4,192,128]{2,1,0:T(8,128)S(1)}, f32[4,192,128]{2,1,0:T(8,128)S(1)}, u32[]{:S(2)}, u32[]{:S(2)}) collective-permute-start(f32[4,192,128]{2,1,0:T(8,128)S(1)} %get-tuple-element.469), channel_id=1, source_target_pairs={{0,4},{4,8},{8,12},{12,16},{16,20},{20,24},{24,28},{28,32},{32,36}... | collective-permute-start | bytes 1179656 | tf_op jit(solution)/shard_map/while/body/eval_jaxpr/ppermute | solution.py:15
  417.3 16.0 %collective-permute-start.2 = (f32[4,192,128]{2,1,0:T(8,128)S(1)}, f32[4,192,128]{2,1,0:T(8,128)S(1)}, u32[]{:S(2)}, u32[]{:S(2)}) collective-permute-start(f32[4,192,128]{2,1,0:T(8,128)S(1)} %get-tuple-element.468), channel_id=1, source_target_pairs={{4,0},{8,4},{12,8},{16,12},{20,16},{24,20},{28,24},{32,28},{36,32}... | collective-permute-start | bytes 1179656 | tf_op jit(solution)/shard_map/while/body/eval_jaxpr/ppermute | solution.py:18
  422.9 11.5 %copy-start.3 = (f32[8,192,128]{2,1,0:T(8,128)S(1)}, f32[8,192,128]{2,1,0:T(8,128)}, u32[]{:S(2)}) copy-start(f32[8,192,128]{2,1,0:T(8,128)} %get-tuple-element.518) | copy-start | bytes 2359300 | tf_op jit(solution)/shard_map/while
  445.0 12.5 %collective-permute-start.3 = (f32[4,192,128]{2,1,0:T(8,128)S(1)}, f32[4,192,128]{2,1,0:T(8,128)S(1)}, u32[]{:S(2)}, u32[]{:S(2)}) collective-permute-start(f32[4,192,128]{2,1,0:T(8,128)S(1)} %get-tuple-element.469), channel_id=1, source_target_pairs={{0,4},{4,8},{8,12},{12,16},{16,20},{20,24},{24,28},{28,32},{32,36}... | collective-permute-start | bytes 1179656 | tf_op jit(solution)/shard_map/while/body/eval_jaxpr/ppermute | solution.py:15
  450.3 15.4 %collective-permute-start.2 = (f32[4,192,128]{2,1,0:T(8,128)S(1)}, f32[4,192,128]{2,1,0:T(8,128)S(1)}, u32[]{:S(2)}, u32[]{:S(2)}) collective-permute-start(f32[4,192,128]{2,1,0:T(8,128)S(1)} %get-tuple-element.468), channel_id=1, source_target_pairs={{4,0},{8,4},{12,8},{16,12},{20,16},{24,20},{28,24},{32,28},{36,32}... | collective-permute-start | bytes 1179656 | tf_op jit(solution)/shard_map/while/body/eval_jaxpr/ppermute | solution.py:18
  477.3 13.2 %collective-permute-start.3 = (f32[4,192,128]{2,1,0:T(8,128)S(1)}, f32[4,192,128]{2,1,0:T(8,128)S(1)}, u32[]{:S(2)}, u32[]{:S(2)}) collective-permute-start(f32[4,192,128]{2,1,0:T(8,128)S(1)} %get-tuple-element.469), channel_id=1, source_target_pairs={{0,4},{4,8},{8,12},{12,16},{16,20},{20,24},{24,28},{28,32},{32,36}... | collective-permute-start | bytes 1179656 | tf_op jit(solution)/shard_map/while/body/eval_jaxpr/ppermute | solution.py:15
  482.6 11.5 %collective-permute-start.2 = (f32[4,192,128]{2,1,0:T(8,128)S(1)}, f32[4,192,128]{2,1,0:T(8,128)S(1)}, u32[]{:S(2)}, u32[]{:S(2)}) collective-permute-start(f32[4,192,128]{2,1,0:T(8,128)S(1)} %get-tuple-element.468), channel_id=1, source_target_pairs={{4,0},{8,4},{12,8},{16,12},{20,16},{24,20},{28,24},{32,28},{36,32}... | collective-permute-start | bytes 1179656 | tf_op jit(solution)/shard_map/while/body/eval_jaxpr/ppermute | solution.py:18
  505.8 19.3 %collective-permute-start.3 = (f32[4,192,128]{2,1,0:T(8,128)S(1)}, f32[4,192,128]{2,1,0:T(8,128)S(1)}, u32[]{:S(2)}, u32[]{:S(2)}) collective-permute-start(f32[4,192,128]{2,1,0:T(8,128)S(1)} %get-tuple-element.469), channel_id=1, source_target_pairs={{0,4},{4,8},{8,12},{12,16},{16,20},{20,24},{24,28},{28,32},{32,36}... | collective-permute-start | bytes 1179656 | tf_op jit(solution)/shard_map/while/body/eval_jaxpr/ppermute | solution.py:15
  510.5 20.2 %collective-permute-start.2 = (f32[4,192,128]{2,1,0:T(8,128)S(1)}, f32[4,192,128]{2,1,0:T(8,128)S(1)}, u32[]{:S(2)}, u32[]{:S(2)}) collective-permute-start(f32[4,192,128]{2,1,0:T(8,128)S(1)} %get-tuple-element.468), channel_id=1, source_target_pairs={{4,0},{8,4},{12,8},{16,12},{20,16},{24,20},{28,24},{32,28},{36,32}... | collective-permute-start | bytes 1179656 | tf_op jit(solution)/shard_map/while/body/eval_jaxpr/ppermute | solution.py:18
  542.4 10.4 %collective-permute-start.3 = (f32[4,192,128]{2,1,0:T(8,128)S(1)}, f32[4,192,128]{2,1,0:T(8,128)S(1)}, u32[]{:S(2)}, u32[]{:S(2)}) collective-permute-start(f32[4,192,128]{2,1,0:T(8,128)S(1)} %get-tuple-element.469), channel_id=1, source_target_pairs={{0,4},{4,8},{8,12},{12,16},{16,20},{20,24},{24,28},{28,32},{32,36}... | collective-permute-start | bytes 1179656 | tf_op jit(solution)/shard_map/while/body/eval_jaxpr/ppermute | solution.py:15
  547.3 16.4 %collective-permute-start.2 = (f32[4,192,128]{2,1,0:T(8,128)S(1)}, f32[4,192,128]{2,1,0:T(8,128)S(1)}, u32[]{:S(2)}, u32[]{:S(2)}) collective-permute-start(f32[4,192,128]{2,1,0:T(8,128)S(1)} %get-tuple-element.468), channel_id=1, source_target_pairs={{4,0},{8,4},{12,8},{16,12},{20,16},{24,20},{28,24},{32,28},{36,32}... | collective-permute-start | bytes 1179656 | tf_op jit(solution)/shard_map/while/body/eval_jaxpr/ppermute | solution.py:18
  553.0 11.7 %copy-start.3 = (f32[8,192,128]{2,1,0:T(8,128)S(1)}, f32[8,192,128]{2,1,0:T(8,128)}, u32[]{:S(2)}) copy-start(f32[8,192,128]{2,1,0:T(8,128)} %get-tuple-element.518) | copy-start | bytes 2359300 | tf_op jit(solution)/shard_map/while
  575.4 12.3 %collective-permute-start.3 = (f32[4,192,128]{2,1,0:T(8,128)S(1)}, f32[4,192,128]{2,1,0:T(8,128)S(1)}, u32[]{:S(2)}, u32[]{:S(2)}) collective-permute-start(f32[4,192,128]{2,1,0:T(8,128)S(1)} %get-tuple-element.469), channel_id=1, source_target_pairs={{0,4},{4,8},{8,12},{12,16},{16,20},{20,24},{24,28},{28,32},{32,36}... | collective-permute-start | bytes 1179656 | tf_op jit(solution)/shard_map/while/body/eval_jaxpr/ppermute | solution.py:15
  580.3 15.4 %collective-permute-start.2 = (f32[4,192,128]{2,1,0:T(8,128)S(1)}, f32[4,192,128]{2,1,0:T(8,128)S(1)}, u32[]{:S(2)}, u32[]{:S(2)}) collective-permute-start(f32[4,192,128]{2,1,0:T(8,128)S(1)} %get-tuple-element.468), channel_id=1, source_target_pairs={{4,0},{8,4},{12,8},{16,12},{20,16},{24,20},{28,24},{32,28},{36,32}... | collective-permute-start | bytes 1179656 | tf_op jit(solution)/shard_map/while/body/eval_jaxpr/ppermute | solution.py:18
  607.4 13.2 %collective-permute-start.3 = (f32[4,192,128]{2,1,0:T(8,128)S(1)}, f32[4,192,128]{2,1,0:T(8,128)S(1)}, u32[]{:S(2)}, u32[]{:S(2)}) collective-permute-start(f32[4,192,128]{2,1,0:T(8,128)S(1)} %get-tuple-element.469), channel_id=1, source_target_pairs={{0,4},{4,8},{8,12},{12,16},{16,20},{20,24},{24,28},{28,32},{32,36}... | collective-permute-start | bytes 1179656 | tf_op jit(solution)/shard_map/while/body/eval_jaxpr/ppermute | solution.py:15
  612.7 11.5 %collective-permute-start.2 = (f32[4,192,128]{2,1,0:T(8,128)S(1)}, f32[4,192,128]{2,1,0:T(8,128)S(1)}, u32[]{:S(2)}, u32[]{:S(2)}) collective-permute-start(f32[4,192,128]{2,1,0:T(8,128)S(1)} %get-tuple-element.468), channel_id=1, source_target_pairs={{4,0},{8,4},{12,8},{16,12},{20,16},{24,20},{28,24},{32,28},{36,32}... | collective-permute-start | bytes 1179656 | tf_op jit(solution)/shard_map/while/body/eval_jaxpr/ppermute | solution.py:18
  635.9 19.3 %collective-permute-start.3 = (f32[4,192,128]{2,1,0:T(8,128)S(1)}, f32[4,192,128]{2,1,0:T(8,128)S(1)}, u32[]{:S(2)}, u32[]{:S(2)}) collective-permute-start(f32[4,192,128]{2,1,0:T(8,128)S(1)} %get-tuple-element.469), channel_id=1, source_target_pairs={{0,4},{4,8},{8,12},{12,16},{16,20},{20,24},{24,28},{28,32},{32,36}... | collective-permute-start | bytes 1179656 | tf_op jit(solution)/shard_map/while/body/eval_jaxpr/ppermute | solution.py:15
  640.6 20.2 %collective-permute-start.2 = (f32[4,192,128]{2,1,0:T(8,128)S(1)}, f32[4,192,128]{2,1,0:T(8,128)S(1)}, u32[]{:S(2)}, u32[]{:S(2)}) collective-permute-start(f32[4,192,128]{2,1,0:T(8,128)S(1)} %get-tuple-element.468), channel_id=1, source_target_pairs={{4,0},{8,4},{12,8},{16,12},{20,16},{24,20},{28,24},{32,28},{36,32}... | collective-permute-start | bytes 1179656 | tf_op jit(solution)/shard_map/while/body/eval_jaxpr/ppermute | solution.py:18
  (50 other events, 216.6 us)
Sparse Core Ops, SparseCore 0:
  672.6 72.8 all-gather.2
